TPU v7x, 256 devices: a whole 4x4x8 slice. The times are simulated.
256 devices in a mesh: rows: 16 (over z_lo, y), cols: 16 (over z_hi, x, core).
Axes of the slice: x: 4, y: 4, z: 8 (z_hi: 2, z_lo: 4; z = z_hi * 4 + z_lo), core: 2. Of those that a mesh axis runs over, the one named last changes fastest.
Arguments:
- patches: bfloat16 [384, 384, 1280], P('rows', 'cols'), may hold values from -6 to 6
- conv_taps: float32 [3, 3, 1280], replicated, may hold values from -1.5 to 1.5
- conv_bias: float32 [1280], replicated, may hold values from -3 to 3
- norm_gain: float32 [1280], replicated, may hold values from 0.1 to 1.9
- norm_bias: float32 [1280], replicated, may hold values from -3 to 3
- qkv_weight: bfloat16 [3, 1280, 1280], P(None, None, 'cols'), may hold values from -0.15625 to 0.15625
- qkv_bias: bfloat16 [3, 1280], P(None, 'cols'), may hold values from -3 to 3
Outputs:
- qkv_heads: bfloat16 [3, 16, 384, 30720], P(None, 'cols', 'rows')
All inputs are finite; a program needn't handle non-finite values.
Results may differ from a plain program's by a relative error of at most 0.0047.
Values may be sent and summed in bfloat16 or wider, within the bound.
A program may use at most 128 MiB of HBM per device.

v0:
```python
import jax
import jax.numpy as jnp
from jax import lax
from jax.sharding import PartitionSpec as P

HD = 80


def with_halo(cells, sides, width):
    for axis, dim in sides:
        count = lax.axis_size(axis)
        ends = count - 1
        head = lax.slice_in_dim(cells, 0, width, axis=dim)
        tail = lax.slice_in_dim(cells, cells.shape[dim] - width, cells.shape[dim], axis=dim)
        cells = jnp.concatenate(
            [
                lax.ppermute(tail, axis, [(i, (i + 1) % count) for i in range(ends)]),
                cells,
                lax.ppermute(head, axis, [((i + 1) % count, i) for i in range(ends)]),
            ],
            axis=dim,
        )
    return cells


def local(patches, conv_taps, conv_bias, norm_gain, norm_bias, qkv_weight, qkv_bias):
    tile_rows, tile_cols, width = patches.shape
    padded = with_halo(patches, (("rows", 0), ("cols", 1)), 1)
    mixed = patches.astype(jnp.float32) + conv_bias
    for a in range(3):
        for b in range(3):
            mixed = mixed + conv_taps[a, b] * padded[a : a + tile_rows, b : b + tile_cols].astype(
                jnp.float32
            )
    mean = jnp.mean(mixed, axis=-1, keepdims=True)
    var = jnp.mean((mixed - mean) ** 2, axis=-1, keepdims=True)
    normed = ((mixed - mean) / jnp.sqrt(var + 1e-06) * norm_gain + norm_bias).astype(jnp.bfloat16)
    own_heads = qkv_weight.shape[2] // HD
    weight_own = qkv_weight.reshape(3, width, own_heads, HD)
    bias_own = qkv_bias.astype(jnp.float32).reshape(3, own_heads, 1, 1, HD)
    out = jnp.einsum(
        "rcd,tdhe->thrce",
        lax.all_gather(normed, "cols", axis=1, tiled=True),
        weight_own,
        preferred_element_type=jnp.float32,
    )
    result = (out + bias_own).astype(jnp.bfloat16)
    return result.reshape(3, result.shape[1], tile_rows, result.shape[3] * HD)


def solution(mesh):
    placed = (P("rows", "cols", None), P(), P(), P(), P(), P(None, None, "cols"), P(None, "cols"))
    return jax.shard_map(
        local, mesh=mesh, in_specs=placed, out_specs=P(None, "cols", "rows", None), check_vma=False
    )
```

profile of v0, /device:TPU:33, one launch (start us, length us, event | category | flops | bytes accessed | tf_op | source)
XLA Modules:
  0.0 314.6 jit_solution(9024591086209875277)
XLA Ops:
  6.5 0.0 copy-start
  6.5 0.0 copy-start.1
  6.5 0.0 copy-start.2
  6.5 0.0 copy-start.3
  6.5 0.0 all-gather.2.cloned.1.call-start
  6.6 1.0 fusion.23
  7.6 3.2 %collective-permute-start = (bf16[1,24,1280]{2,1,0:T(8,128)(2,1)S(1)}, bf16[1,24,1280]{2,1,0:T(8,128)(2,1)S(1)}, u32[]{:S(2)}, u32[]{:S(2)}) collective-permute-start(bf16[1,24,1280]{2,1,0:T(8,128)(2,1)S(1)} %get-tuple-element.19), channel_id=1, source_target_pairs={{0,16},{16,32},{32,48},{48,64},{64,80},{80,96},{96,112},{112,128},... | collective-permute-start | bytes 184328 | tf_op jit(solution)/shard_map/ppermute | solution.py:17
  10.8 4.2 %collective-permute-start.1 = (bf16[1,24,1280]{2,1,0:T(8,128)(2,1)S(1)}, bf16[1,24,1280]{2,1,0:T(8,128)(2,1)S(1)}, u32[]{:S(2)}, u32[]{:S(2)}) collective-permute-start(bf16[1,24,1280]{2,1,0:T(8,128)(2,1)S(1)} %get-tuple-element.18), channel_id=1, source_target_pairs={{16,0},{32,16},{48,32},{64,48},{80,64},{96,80},{112,96},{128,112},... | collective-permute-start | bytes 184328 | tf_op jit(solution)/shard_map/ppermute | solution.py:19
  15.0 0.0 collective-permute-done
  15.0 1.5 constant_dynamic-update-slice_fusion.1
  16.5 0.0 collective-permute-done.1
  16.5 0.2 fusion.22
  16.7 4.6 %collective-permute-start.2 = (bf16[26,1,1280]{2,1,0:T(2,128)(2,1)S(1)}, bf16[26,1,1280]{2,1,0:T(2,128)(2,1)S(1)}, u32[]{:S(2)}, u32[]{:S(2)}) collective-permute-start(bf16[26,1,1280]{2,1,0:T(2,128)(2,1)S(1)} %get-tuple-element.16), channel_id=1, source_target_pairs={{0,1},{1,2},{2,3},{3,4},{4,5},{5,6},{6,7},{7,8},{8,9},{9,10},{10,1... | collective-permute-start | bytes 199688 | tf_op jit(solution)/shard_map/ppermute | solution.py:17
  21.3 1.9 collective-permute-start.3
  23.2 0.0 copy-done.2
  23.3 0.1 slice_reduce_fusion.8
  23.4 0.0 collective-permute-done.2
  23.4 4.2 %collective-permute-done.3 = bf16[26,1,1280]{2,1,0:T(2,128)(2,1)S(1)} collective-permute-done((bf16[26,1,1280]{2,1,0:T(2,128)(2,1)S(1)}, bf16[26,1,1280]{2,1,0:T(2,128)(2,1)S(1)}, u32[]{:S(2)}, u32[]{:S(2)}) %collective-permute-start.3) | collective-permute-done | bytes 66592 | tf_op jit(solution)/shard_map/ppermute | solution.py:19
  27.6 0.0 copy-done.1
  27.6 0.0 copy-done.3
  27.6 5.9 %fusion.20 = (f32[24,24]{1,0:T(8,128)S(1)}, f32[24,24,1280]{2,1,0:T(8,128)S(1)}) fusion(bf16[26,1,1280]{2,1,0:T(2,128)(2,1)S(1)} %collective-permute-done.3, bf16[26,24,1280]{2,1,0:T(8,128)(2,1)S(1)} %constant_dynamic-update-slice_fusion, f32[1280]{0:T(1024)S(1)} %get-tuple-element.12, bf16[1,24,1280]{2,1,0:T(8,128)(2,1)S(1)} %collective-permute-done.1, ...), kind=kLoop, calls=%fused_computation.49 | loop fusion | flops 39075264 | bytes 6330624 | tf_op jit(solution)/shard_map/reduce_sum | solution.py:35
  33.5 0.0 copy-start.4
  33.6 0.0 copy-start.5
  33.6 0.4 multiply_reduce_fusion
  34.0 0.2 copy-done.4
  34.2 0.0 copy-done.5
  34.3 0.0 copy-start.6
  34.3 1.6 add_convert_fusion
  35.9 0.0 all-gather.2.cloned.1.call-update
  35.9 0.0 copy-done.6
  36.0 237.6 %all-gather.2.cloned.1.call-done = bf16[24,384,1280]{2,1,0:T(8,128)(2,1)} async-done(((bf16[24,24,1280]{2,1,0:T(8,128)(2,1)}), bf16[24,384,1280]{2,1,0:T(8,128)(2,1)}) %all-gather.2.cloned.1.call-update) | async-done | bytes 23592976 | tf_op jit(solution)/shard_map/all_gather | solution.py:43
  273.6 0.0 copy-done
  273.6 12.3 %fusion.3 = bf16[3,1,24,384,80]{3,4,0,2,1:T(8,128)(2,1)} fusion(f32[3,80]{1,0:T(4,128)S(1)} %convert_element_type.50, bf16[24,384,1280]{2,1,0:T(8,128)(2,1)} %all-gather.2.cloned.1.call-done, bf16[3,1280,80]{1,2,0:T(8,128)(2,1)S(1)} %copy-done), kind=kOutput, calls=%fused_computation.4 | convolution fusion | flops 5666734080 | bytes 28632000 | tf_op jit(solution)/shard_map/rcd,tdhe->thrce/dot_general | solution.py:41
  285.9 8.1 %copy.8 = bf16[3,1,24,384,80]{4,3,2,0,1:T(8,128)(2,1)} copy(bf16[3,1,24,384,80]{3,4,0,2,1:T(8,128)(2,1)} %fusion.3) | data formatting | bytes 8847360 | tf_op jit(solution)/shard_map/convert_element_type | solution.py:47
  294.0 13.7 %reshape.26 = bf16[3,1,24,30720]{3,2,0,1:T(8,128)(2,1)} reshape(bf16[3,1,24,384,80]{4,3,2,0,1:T(8,128)(2,1)} %copy.8) | data formatting | bytes 8847360 | tf_op jit(solution)/shard_map/reshape | solution.py:48
  (5 shorter events, 0.0 us)
Async XLA Ops:
  6.5 267.0 %copy-start = (bf16[3,1280,80]{1,2,0:T(8,128)(2,1)S(1)}, bf16[3,1280,80]{1,2,0:T(8,128)(2,1)}, u32[]{:S(2)}) copy-start(bf16[3,1280,80]{1,2,0:T(8,128)(2,1)} %param.12) | copy-start | bytes 1843204
  6.5 21.1 %copy-start.1 = (bf16[24,24,1280]{2,1,0:T(8,128)(2,1)S(1)}, bf16[24,24,1280]{2,1,0:T(8,128)(2,1)}, u32[]{:S(2)}) copy-start(bf16[24,24,1280]{2,1,0:T(8,128)(2,1)} %param.7) | copy-start | bytes 4423684
  6.5 16.7 %copy-start.2 = (f32[3,3,1280]{2,1,0:T(4,128)S(1)}, f32[3,3,1280]{2,1,0:T(4,128)}, u32[]{:S(2)}) copy-start(f32[3,3,1280]{2,1,0:T(4,128)} %param.8) | copy-start | bytes 138244
  6.5 21.1 %copy-start.3 = (f32[1280]{0:T(1024)S(1)}, f32[1280]{0:T(1024)}, u32[]{:S(2)}) copy-start(f32[1280]{0:T(1024)} %param.9) | copy-start | bytes 15364
  6.5 267.0 %all-gather.2.cloned.1.call-start = ((), (), s32[]{:S(2)}) async-start(), calls=%async_computation | async-start | bytes 25067520 | tf_op jit(solution)/shard_map/all_gather | solution.py:43
  7.6 7.4 %collective-permute-start = (bf16[1,24,1280]{2,1,0:T(8,128)(2,1)S(1)}, bf16[1,24,1280]{2,1,0:T(8,128)(2,1)S(1)}, u32[]{:S(2)}, u32[]{:S(2)}) collective-permute-start(bf16[1,24,1280]{2,1,0:T(8,128)(2,1)S(1)} %get-tuple-element.19), channel_id=1, source_target_pairs={{0,16},{16,32},{32,48},{48,64},{64,80},{80,96},{96,112},{112,128},... | collective-permute-start | bytes 184328 | tf_op jit(solution)/shard_map/ppermute | solution.py:17
  10.8 5.7 %collective-permute-start.1 = (bf16[1,24,1280]{2,1,0:T(8,128)(2,1)S(1)}, bf16[1,24,1280]{2,1,0:T(8,128)(2,1)S(1)}, u32[]{:S(2)}, u32[]{:S(2)}) collective-permute-start(bf16[1,24,1280]{2,1,0:T(8,128)(2,1)S(1)} %get-tuple-element.18), channel_id=1, source_target_pairs={{16,0},{32,16},{48,32},{64,48},{80,64},{96,80},{112,96},{128,112},... | collective-permute-start | bytes 184328 | tf_op jit(solution)/shard_map/ppermute | solution.py:19
  16.7 6.6 %collective-permute-start.2 = (bf16[26,1,1280]{2,1,0:T(2,128)(2,1)S(1)}, bf16[26,1,1280]{2,1,0:T(2,128)(2,1)S(1)}, u32[]{:S(2)}, u32[]{:S(2)}) collective-permute-start(bf16[26,1,1280]{2,1,0:T(2,128)(2,1)S(1)} %get-tuple-element.16), channel_id=1, source_target_pairs={{0,1},{1,2},{2,3},{3,4},{4,5},{5,6},{6,7},{7,8},{8,9},{9,10},{10,1... | collective-permute-start | bytes 199688 | tf_op jit(solution)/shard_map/ppermute | solution.py:17
  21.3 6.3 %collective-permute-start.3 = (bf16[26,1,1280]{2,1,0:T(2,128)(2,1)S(1)}, bf16[26,1,1280]{2,1,0:T(2,128)(2,1)S(1)}, u32[]{:S(2)}, u32[]{:S(2)}) collective-permute-start(bf16[26,1,1280]{2,1,0:T(2,128)(2,1)S(1)} %get-tuple-element.17), channel_id=1, source_target_pairs={{1,0},{2,1},{3,2},{4,3},{5,4},{6,5},{7,6},{8,7},{9,8},{10,9},{11,1... | collective-permute-start | bytes 199688 | tf_op jit(solution)/shard_map/ppermute | solution.py:19
  33.5 0.7 copy-start.4
  33.6 0.7 copy-start.5
  34.3 1.7 copy-start.6
Sparse Core Ops, SparseCore 0:
  36.0 237.4 all-gather.1
where the time goes:
time: 319 us; the launch traced here: 315 us
  waiting for transfers between devices  242 us (76%)
  local copies, waits for them, and re-layouts  24.9 us (8%)
  starting transfers between devices  13.9 us (4%)
  between operations  13.6 us (4%)
  matrix products  12.3 us (4%)
  other arithmetic  7.99 us (3%)
    all_gather x1, waiting for transfers between devices, local(): lax.all_gather(normed, 'cols', axis=1, tiled=True)  238 us
    reshape x1, local copies, waits for them, and re-layouts, local(): return result.reshape(3, result.shape[1], tile_rows, result.shape[3] * HD)  13.7 us
    dot_general x1, matrix products, local(): jnp.einsum('rcd,tdhe->thrce', lax.all_gather(normed, 'cols', axis=1, tile...  12.3 us
    convert_element_type x1, local copies, waits for them, and re-layouts, local(): result = (out + bias_own).astype(jnp.bfloat16)  8.1 us
    ppermute x2, starting transfers between devices, with_halo(): lax.ppermute(tail, axis, [(i, (i + 1) % count) for i in range(ends)])  7.77 us
  transfers between devices with their start and end apart: 5, of which 2 were waited for; matrix products, arithmetic and copies ran while one was open for 1% of the time, Pallas kernels for 0%

commit v1 on v0

v1 whole, which is shorter than its diff:
```python
import jax
import jax.numpy as jnp
from jax import lax
from jax.sharding import Mesh, PartitionSpec as P

HD = 80
ROWS = ("zl", "y")
COLS = ("zh", "x", "core")
SIDE = ("x", "core")


def with_halo(cells, sides, width):
    for axis, dim in sides:
        count = lax.axis_size(axis)
        ends = count - 1
        head = lax.slice_in_dim(cells, 0, width, axis=dim)
        tail = lax.slice_in_dim(cells, cells.shape[dim] - width, cells.shape[dim], axis=dim)
        cells = jnp.concatenate(
            [
                lax.ppermute(tail, axis, [(i, (i + 1) % count) for i in range(ends)]),
                cells,
                lax.ppermute(head, axis, [((i + 1) % count, i) for i in range(ends)]),
            ],
            axis=dim,
        )
    return cells


def local(patches, conv_taps, conv_bias, norm_gain, norm_bias, qkv_weight, qkv_bias):
    tile_rows, tile_cols, width = patches.shape
    padded = with_halo(patches, ((ROWS, 0), (COLS, 1)), 1)
    mixed = patches.astype(jnp.float32) + conv_bias
    for a in range(3):
        for b in range(3):
            mixed = mixed + conv_taps[a, b] * padded[a : a + tile_rows, b : b + tile_cols].astype(
                jnp.float32
            )
    mean = jnp.mean(mixed, axis=-1, keepdims=True)
    var = jnp.mean((mixed - mean) ** 2, axis=-1, keepdims=True)
    normed = ((mixed - mean) / jnp.sqrt(var + 1e-06) * norm_gain + norm_bias).astype(jnp.bfloat16)
    pair = lax.all_gather(normed, "zh", axis=0, tiled=False)
    weight_side = lax.all_gather(qkv_weight, SIDE, axis=2, tiled=True)
    bias_side = lax.all_gather(qkv_bias, SIDE, axis=1, tiled=True)
    heads = weight_side.shape[2] // HD
    weight_side = weight_side.reshape(3, width, heads, HD)
    bias_side = bias_side.astype(jnp.float32).reshape(3, heads, 1, 1, 1, HD)
    out = jnp.einsum("jrcd,tdhe->thjrce", pair, weight_side, preferred_element_type=jnp.float32)
    out = (out + bias_side).astype(jnp.bfloat16)
    got = lax.all_to_all(out, SIDE, 1, 1, tiled=True)
    got = jnp.transpose(got, (0, 3, 2, 1, 4, 5))
    return got.reshape(3, 1, tile_rows, -1)


def solution(mesh):
    fine = Mesh(mesh.devices.reshape(4, 4, 2, 4, 2), ROWS + COLS)
    placed = (P(ROWS, COLS, None), P(), P(), P(), P(), P(None, None, COLS), P(None, COLS))
    return jax.shard_map(
        local, mesh=fine, in_specs=placed, out_specs=P(None, COLS, ROWS, None), check_vma=False
    )
```

time: 319 us -> 292 us (0.915)
  waiting for transfers between devices: 242 us -> 115 us
  blocking collectives: 0 us -> 103 us
    all_gather x1 -> x2, waiting for transfers between devices: 238 us -> 109 us  [the longest x1 71.5 us: local(): pair = lax.all_gather(normed, 'zh', axis=0, tiled=False)]
    all_to_all x0 -> x1, blocking collectives: none -> 83.7 us  [local(): got = lax.all_to_all(out, SIDE, 1, 1, tiled=True)]
    all_gather x0 -> x1, blocking collectives: none -> 19.3 us  [local(): bias_side = lax.all_gather(qkv_bias, SIDE, axis=1, tiled=True)]
    transpose x0 -> x1, local copies, waits for them, and re-layouts: none -> 4.95 us  [local(): got = jnp.transpose(got, (0, 3, 2, 1, 4, 5))]
    convert_element_type x1 -> x2, local copies, waits for them, and re-layouts: 8.1 us -> 3.18 us  [the longest x1 1.82 us: local(): out = (out + bias_side).astype(jnp.bfloat16)]
  transfers between devices with their start and end apart: 5 -> 6, of which waited for: 2 -> 5; matrix products, arithmetic and copies ran while one was open for 1% -> 0% of each run, Pallas kernels for 0% -> 0%
where the time goes in v1:
time: 292 us; the launch traced here: 290 us
  waiting for transfers between devices  115 us (39%)
  blocking collectives  103 us (35%)
  local copies, waits for them, and re-layouts  24.2 us (8%)
  starting transfers between devices  14.2 us (5%)
  between operations  13.6 us (5%)
  matrix products  12.2 us (4%)
  other arithmetic  8.16 us (3%)
    all_to_all x1, blocking collectives, local(): got = lax.all_to_all(out, SIDE, 1, 1, tiled=True)  83.7 us
    all_gather x1, waiting for transfers between devices, local(): pair = lax.all_gather(normed, 'zh', axis=0, tiled=False)  71.5 us
    all_gather x1, waiting for transfers between devices, local(): weight_side = lax.all_gather(qkv_weight, SIDE, axis=2, tiled=True)  37.4 us
    all_gather x1, blocking collectives, local(): bias_side = lax.all_gather(qkv_bias, SIDE, axis=1, tiled=True)  19.3 us
    reshape x1, local copies, waits for them, and re-layouts, local(): return got.reshape(3, 1, tile_rows, -1)  13.7 us
    dot_general x1, matrix products, local(): jnp.einsum('jrcd,tdhe->thjrce', pair, weight_side, preferred_element_type...  12.2 us
    ppermute x2, starting transfers between devices, with_halo(): lax.ppermute(tail, axis, [(i, (i + 1) % count) for i in range(ends)])  8.02 us
    ppermute x2, starting transfers between devices, with_halo(): lax.ppermute(head, axis, [((i + 1) % count, i) for i in range(ends)])  6.11 us
  transfers between devices with their start and end apart: 6, of which 5 were waited for; matrix products, arithmetic and copies ran while one was open for 0% of the time, Pallas kernels for 0%

profile of v1, /device:TPU:33, one launch (start us, length us, event | category | flops | bytes accessed | tf_op | source)
XLA Modules:
  0.0 290.3 jit_solution(11182226161861698135)
XLA Ops:
  6.5 0.0 copy-start
  6.5 0.0 all-gather.7.cloned.1.call-start
  6.5 1.6 copy.22
  8.2 0.2 fusion.12
  8.4 3.2 %collective-permute-start = (bf16[1,24,1280]{2,0,1:T(2,128)(2,1)S(1)}, bf16[1,24,1280]{2,0,1:T(2,128)(2,1)S(1)}, u32[]{:S(2)}, u32[]{:S(2)}) collective-permute-start(bf16[1,24,1280]{2,0,1:T(2,128)(2,1)S(1)} %get-tuple-element.20), channel_id=1, source_target_pairs={{0,16},{16,32},{32,48},{48,64},{64,80},{80,96},{96,112},{112,128},... | collective-permute-start | bytes 184328 | tf_op jit(solution)/shard_map/ppermute | solution.py:20
  11.6 4.2 %collective-permute-start.1 = (bf16[1,24,1280]{2,0,1:T(2,128)(2,1)S(1)}, bf16[1,24,1280]{2,0,1:T(2,128)(2,1)S(1)}, u32[]{:S(2)}, u32[]{:S(2)}) collective-permute-start(bf16[1,24,1280]{2,0,1:T(2,128)(2,1)S(1)} %get-tuple-element.21), channel_id=1, source_target_pairs={{16,0},{32,16},{48,32},{64,48},{80,64},{96,80},{112,96},{128,112},... | collective-permute-start | bytes 184328 | tf_op jit(solution)/shard_map/ppermute | solution.py:22
  15.8 0.8 collective-permute-done
  16.6 1.1 collective-permute-done.1
  17.6 0.1 pad_maximum_fusion.5
  17.7 4.8 %collective-permute-start.2 = (bf16[26,1,1280]{2,0,1:T(8,128)(2,1)S(1)}, bf16[26,1,1280]{2,0,1:T(8,128)(2,1)S(1)}, u32[]{:S(2)}, u32[]{:S(2)}) collective-permute-start(bf16[26,1,1280]{2,0,1:T(8,128)(2,1)S(1)} %get-tuple-element.18), channel_id=1, source_target_pairs={{0,1},{1,2},{2,3},{3,4},{4,5},{5,6},{6,7},{7,8},{8,9},{9,10},{10,1... | collective-permute-start | bytes 199688 | tf_op jit(solution)/shard_map/ppermute | solution.py:20
  22.5 1.9 collective-permute-start.3
  24.4 0.0 copy-done
  24.5 0.1 slice_reduce_fusion.8
  24.6 0.0 copy-start.3
  24.6 0.0 collective-permute-done.2
  24.6 3.7 %collective-permute-done.3 = bf16[26,1,1280]{2,0,1:T(8,128)(2,1)S(1)} collective-permute-done((bf16[26,1,1280]{2,0,1:T(8,128)(2,1)S(1)}, bf16[26,1,1280]{2,0,1:T(8,128)(2,1)S(1)}, u32[]{:S(2)}, u32[]{:S(2)}) %collective-permute-start.3) | collective-permute-done | bytes 66592 | tf_op jit(solution)/shard_map/ppermute | solution.py:22
  28.3 2.4 maximum_maximum_fusion
  30.7 0.0 copy-done.3
  30.7 4.8 %fusion.10 = (f32[24,24]{0,1:T(8,128)S(1)}, f32[24,24,1280]{2,0,1:T(8,128)S(1)}) fusion(bf16[26,25,1280]{2,0,1:T(8,128)(2,1)S(1)} %get-tuple-element.17, f32[1280]{0:T(1024)S(1)} %get-tuple-element.12, bf16[1,24,1280]{2,0,1:T(2,128)(2,1)S(1)} %collective-permute-done.1, bf16[24,24,1280]{2,0,1:T(8,128)(2,1)S(1)} %copy.22, f32[1280]{0:T(1024)S(1)} %get-tuple-element.13, ...), kind=kLoop, calls=%fused_computation.34 | loop fusion | flops 25804224 | bytes 13447424 | tf_op jit(solution)/shard_map/reduce_sum | solution.py:38
  35.4 0.0 copy-start.1
  35.5 0.0 copy-start.2
  35.5 0.4 multiply_reduce_fusion
  35.9 0.2 copy-done.1
  36.1 0.0 copy-done.2
  36.2 0.5 add_convert_fusion.1
  36.7 0.0 copy-start.4
  36.7 1.4 copy.28
  38.1 0.0 all-gather.7.cloned.1.call-update
  38.1 0.0 all-gather.5.cloned.1.call-start
  38.1 0.7 all-gather.5.cloned.1.call-update
  38.8 0.0 copy-done.4
  38.9 19.3 %all-gather.1 = bf16[8,80,3]{1,2,0:T(4,128)(2,1)S(1)} all-gather(bf16[1,80,3]{1,2,0:T(4,128)(2,1)S(1)} %bitcast.26), channel_id=1, replica_groups=mesh['zl'=4,'y'=4,'zh'=2,'x'=4,'core'=2] {'x','core'}, dimensions={0}, use_global_device_ids=true | all-gather | bytes 4320 | tf_op jit(solution)/shard_map/all_gather | solution.py:43
  58.1 0.1 reshape.29
  58.2 0.1 reshape.25
  58.3 71.5 %all-gather.7.cloned.1.call-done = bf16[48,24,1280]{2,1,0:T(8,128)(2,1)} async-done(((bf16[24,24,1280]{2,1,0:T(8,128)(2,1)}), bf16[48,24,1280]{2,1,0:T(8,128)(2,1)}) %all-gather.7.cloned.1.call-update) | async-done | bytes 2949136 | tf_op jit(solution)/shard_map/all_gather | solution.py:41
  129.8 37.4 %all-gather.5.cloned.1.call-done = bf16[3,1280,640]{1,2,0:T(8,128)(2,1)} async-done(((bf16[3,1280,80]{1,2,0:T(8,128)(2,1)}), bf16[3,1280,640]{1,2,0:T(8,128)(2,1)}) %all-gather.5.cloned.1.call-update) | async-done | bytes 4915216 | tf_op jit(solution)/shard_map/all_gather | solution.py:42
  167.1 12.2 %fusion = bf16[3,8,2,24,24,80]{5,4,1,0,3,2:T(8,128)(2,1)S(1)} fusion(f32[3,8,80]{2,1,0:T(8,128)S(1)} %reshape.25, bf16[2,24,24,1280,1,1]{3,2,5,4,1,0:T(8,128)(2,1)} %bitcast.28, bf16[3,1280,8,80,1,1]{1,3,2,0,5,4:T(8,128)(2,1)} %bitcast.27), kind=kOutput, calls=%fused_computation.1 | convolution fusion | flops 5666734080 | bytes 12295680 | tf_op jit(solution)/shard_map/jrcd,tdhe->thjrce/dot_general | solution.py:47
  179.3 1.8 copy.30
  181.1 83.7 %all_to_all.5 = bf16[3,8,2,24,24,80]{5,4,0,3,2,1:T(8,128)(2,1)S(1)} all-to-all(bf16[3,8,2,24,24,80]{5,4,0,3,2,1:T(8,128)(2,1)S(1)} %copy.30), channel_id=1, replica_groups=mesh['zl'=4,'y'=4,'zh'=2,'x'=4,'core'=2] {'x','core'}, dimensions={1} | all-to-all | bytes 8847360 | tf_op jit(solution)/shard_map/all_to_all | solution.py:49
  264.8 4.9 %copy.31 = bf16[3,24,2,8,24,80]{5,4,3,2,1,0:T(8,128)(2,1)} copy(bf16[3,24,2,8,24,80]{5,4,0,1,2,3:T(8,128)(2,1)S(1)} %bitcast.24) | data formatting | bytes 8847360 | tf_op jit(solution)/shard_map/transpose | solution.py:50
  269.8 13.7 %reshape.24 = bf16[3,1,24,30720]{3,2,0,1:T(8,128)(2,1)} reshape(bf16[3,24,2,8,24,80]{5,4,3,2,1,0:T(8,128)(2,1)} %copy.31) | data formatting | bytes 8847360 | tf_op jit(solution)/shard_map/reshape | solution.py:51
  (3 shorter events, 0.0 us)
Async XLA Ops:
  6.5 17.9 %copy-start = (f32[3,3,1280]{2,1,0:T(4,128)S(1)}, f32[3,3,1280]{2,1,0:T(4,128)}, u32[]{:S(2)}) copy-start(f32[3,3,1280]{2,1,0:T(4,128)} %param.8) | copy-start | bytes 138244
  6.5 123.2 %all-gather.7.cloned.1.call-start = ((), (), s32[]{:S(2)}) async-start(), calls=%async_computation.2 | async-start | bytes 4423680 | tf_op jit(solution)/shard_map/all_gather | solution.py:41
  8.4 8.2 %collective-permute-start = (bf16[1,24,1280]{2,0,1:T(2,128)(2,1)S(1)}, bf16[1,24,1280]{2,0,1:T(2,128)(2,1)S(1)}, u32[]{:S(2)}, u32[]{:S(2)}) collective-permute-start(bf16[1,24,1280]{2,0,1:T(2,128)(2,1)S(1)} %get-tuple-element.20), channel_id=1, source_target_pairs={{0,16},{16,32},{32,48},{48,64},{64,80},{80,96},{96,112},{112,128},... | collective-permute-start | bytes 184328 | tf_op jit(solution)/shard_map/ppermute | solution.py:20
  11.6 6.0 %collective-permute-start.1 = (bf16[1,24,1280]{2,0,1:T(2,128)(2,1)S(1)}, bf16[1,24,1280]{2,0,1:T(2,128)(2,1)S(1)}, u32[]{:S(2)}, u32[]{:S(2)}) collective-permute-start(bf16[1,24,1280]{2,0,1:T(2,128)(2,1)S(1)} %get-tuple-element.21), channel_id=1, source_target_pairs={{16,0},{32,16},{48,32},{64,48},{80,64},{96,80},{112,96},{128,112},... | collective-permute-start | bytes 184328 | tf_op jit(solution)/shard_map/ppermute | solution.py:22
  17.7 6.9 %collective-permute-start.2 = (bf16[26,1,1280]{2,0,1:T(8,128)(2,1)S(1)}, bf16[26,1,1280]{2,0,1:T(8,128)(2,1)S(1)}, u32[]{:S(2)}, u32[]{:S(2)}) collective-permute-start(bf16[26,1,1280]{2,0,1:T(8,128)(2,1)S(1)} %get-tuple-element.18), channel_id=1, source_target_pairs={{0,1},{1,2},{2,3},{3,4},{4,5},{5,6},{6,7},{7,8},{8,9},{9,10},{10,1... | collective-permute-start | bytes 199688 | tf_op jit(solution)/shard_map/ppermute | solution.py:20
  22.5 5.8 %collective-permute-start.3 = (bf16[26,1,1280]{2,0,1:T(8,128)(2,1)S(1)}, bf16[26,1,1280]{2,0,1:T(8,128)(2,1)S(1)}, u32[]{:S(2)}, u32[]{:S(2)}) collective-permute-start(bf16[26,1,1280]{2,0,1:T(8,128)(2,1)S(1)} %get-tuple-element.19), channel_id=1, source_target_pairs={{1,0},{2,1},{3,2},{4,3},{5,4},{6,5},{7,6},{8,7},{9,8},{10,9},{11,1... | collective-permute-start | bytes 199688 | tf_op jit(solution)/shard_map/ppermute | solution.py:22
  24.6 6.1 %copy-start.3 = (f32[1280]{0:T(1024)S(1)}, f32[1280]{0:T(1024)}, u32[]{:S(2)}) copy-start(f32[1280]{0:T(1024)} %param.9) | copy-start | bytes 15364
  35.4 0.7 copy-start.1
  35.5 0.7 copy-start.2
  36.7 2.1 copy-start.4
  38.1 129.0 %all-gather.5.cloned.1.call-start = ((), (), s32[]{:S(2)}) async-start(), calls=%async_computation.1 | async-start | bytes 5529600 | tf_op jit(solution)/shard_map/all_gather | solution.py:42
Sparse Core Ops, SparseCore 0:
  38.2 91.5 all-gather.6
  131.6 35.4 all-gather.4

commit v2 on v1

--- a/solution.py
+++ b/solution.py
@@ -26,8 +26,23 @@
     return cells
 
 
+def project(tile, weight_side, bias_side):
+    out = jnp.einsum("rcd,tdhe->trhce", tile, weight_side, preferred_element_type=jnp.float32)
+    return (out + bias_side).astype(jnp.bfloat16)
+
+
+def deliver(out):
+    return lax.all_to_all(out, SIDE, 2, 2, tiled=True)
+
+
 def local(patches, conv_taps, conv_bias, norm_gain, norm_bias, qkv_weight, qkv_bias):
     tile_rows, tile_cols, width = patches.shape
+    packed = jnp.concatenate([qkv_weight, qkv_bias[:, None, :]], axis=1)
+    packed = lax.all_gather(packed, SIDE, axis=2, tiled=True)
+    heads = packed.shape[2] // HD
+    weight_side = packed[:, :width].reshape(3, width, heads, HD)
+    bias_side = packed[:, width].astype(jnp.float32).reshape(3, 1, heads, 1, HD)
+
     padded = with_halo(patches, ((ROWS, 0), (COLS, 1)), 1)
     mixed = patches.astype(jnp.float32) + conv_bias
     for a in range(3):
@@ -38,16 +53,15 @@
     mean = jnp.mean(mixed, axis=-1, keepdims=True)
     var = jnp.mean((mixed - mean) ** 2, axis=-1, keepdims=True)
     normed = ((mixed - mean) / jnp.sqrt(var + 1e-06) * norm_gain + norm_bias).astype(jnp.bfloat16)
-    pair = lax.all_gather(normed, "zh", axis=0, tiled=False)
-    weight_side = lax.all_gather(qkv_weight, SIDE, axis=2, tiled=True)
-    bias_side = lax.all_gather(qkv_bias, SIDE, axis=1, tiled=True)
-    heads = weight_side.shape[2] // HD
-    weight_side = weight_side.reshape(3, width, heads, HD)
-    bias_side = bias_side.astype(jnp.float32).reshape(3, heads, 1, 1, 1, HD)
-    out = jnp.einsum("jrcd,tdhe->thjrce", pair, weight_side, preferred_element_type=jnp.float32)
-    out = (out + bias_side).astype(jnp.bfloat16)
-    got = lax.all_to_all(out, SIDE, 1, 1, tiled=True)
-    got = jnp.transpose(got, (0, 3, 2, 1, 4, 5))
+    own = project(normed, weight_side, bias_side)
+    normed, own = lax.optimization_barrier((normed, own))
+    partner = lax.ppermute(normed, "zh", [(0, 1), (1, 0)])
+    own = deliver(own)
+    other = deliver(project(partner, weight_side, bias_side))
+    first = lax.axis_index("zh") == 0
+    low = jnp.where(first, own, other)
+    high = jnp.where(first, other, own)
+    got = jnp.stack([low, high], axis=2)
     return got.reshape(3, 1, tile_rows, -1)
 
 

time: 292 us -> 222 us (0.76)
  blocking collectives: 103 us -> 0 us
  starting transfers between devices: 14.2 us -> 29.3 us
  other arithmetic: 8.16 us -> 15.4 us
  local copies, waits for them, and re-layouts: 24.2 us -> 28.8 us
  waiting for transfers between devices: 115 us -> 119 us
    all_gather x2 -> x1, waiting for transfers between devices: 109 us -> 11.1 us  [local(): packed = lax.all_gather(packed, SIDE, axis=2, tiled=True)]
    all_to_all x1 -> x0, blocking collectives: 83.7 us -> none  [local(): got = lax.all_to_all(out, SIDE, 1, 1, tiled=True)]
    ppermute x0 -> x1, waiting for transfers between devices: none -> 57.7 us  [local(): partner = lax.ppermute(normed, 'zh', [(0, 1), (1, 0)])]
    all_to_all x0 -> x2, waiting for transfers between devices: none -> 41.9 us  [deliver(): return lax.all_to_all(out, SIDE, 2, 2, tiled=True)]
    all_gather x1 -> x0, blocking collectives: 19.3 us -> none  [local(): bias_side = lax.all_gather(qkv_bias, SIDE, axis=1, tiled=True)]
    all_to_all x0 -> x2, starting transfers between devices: none -> 9.55 us  [deliver(): return lax.all_to_all(out, SIDE, 2, 2, tiled=True)]
    ppermute x0 -> x1, starting transfers between devices: none -> 5.6 us  [local(): partner = lax.ppermute(normed, 'zh', [(0, 1), (1, 0)])]
    another operation x0 -> x1, local copies, waits for them, and re-layouts: none -> 4.97 us  [local(): got = jnp.stack([low, high], axis=2)]
  transfers between devices with their start and end apart: 6 -> 8, of which waited for: 5 -> 6; matrix products, arithmetic and copies ran while one was open for 0% -> 10% of each run, Pallas kernels for 0% -> 0%
where the time goes in v2:
time: 222 us; the launch traced here: 220 us
  waiting for transfers between devices  119 us (54%)
  starting transfers between devices  29.3 us (13%)
  local copies, waits for them, and re-layouts  28.8 us (13%)
  other arithmetic  15.4 us (7%)
  matrix products  13.8 us (6%)
  between operations  13.6 us (6%)
    ppermute x1, waiting for transfers between devices, local(): partner = lax.ppermute(normed, 'zh', [(0, 1), (1, 0)])  57.7 us
    all_to_all x2, waiting for transfers between devices, deliver(): return lax.all_to_all(out, SIDE, 2, 2, tiled=True)  41.9 us
    dot_general x2, matrix products, project(): jnp.einsum('rcd,tdhe->trhce', tile, weight_side, preferred_element_type=j...  13.8 us
    reshape x1, local copies, waits for them, and re-layouts, local(): return got.reshape(3, 1, tile_rows, -1)  13.7 us
    all_gather x1, waiting for transfers between devices, local(): packed = lax.all_gather(packed, SIDE, axis=2, tiled=True)  11.1 us
    all_to_all x2, starting transfers between devices, deliver(): return lax.all_to_all(out, SIDE, 2, 2, tiled=True)  9.55 us
    ppermute x2, starting transfers between devices, with_halo(): lax.ppermute(tail, axis, [(i, (i + 1) % count) for i in range(ends)])  8.02 us
    ppermute x2, waiting for transfers between devices, with_halo(): lax.ppermute(head, axis, [((i + 1) % count, i) for i in range(ends)])  7.92 us
  transfers between devices with their start and end apart: 8, of which 6 were waited for; matrix products, arithmetic and copies ran while one was open for 10% of the time, Pallas kernels for 0%

profile of v2, /device:TPU:33, one launch (start us, length us, event | category | flops | bytes accessed | tf_op | source)
XLA Modules:
  0.0 220.0 jit_solution(10254981237282934352)
XLA Ops:
  6.5 0.0 copy-start
  6.5 0.0 all-gather.2.cloned.1.call-start
  6.5 0.9 copy.12
  7.5 0.0 copy-start.2
  7.5 0.0 copy-start.3
  7.5 2.0 pad_maximum_fusion.5
  9.5 0.0 all-gather.2.cloned.1.call-update
  9.5 0.9 fusion.20
  10.4 3.2 %collective-permute-start = (bf16[1,24,1280]{2,1,0:T(8,128)(2,1)S(1)}, bf16[1,24,1280]{2,1,0:T(8,128)(2,1)S(1)}, u32[]{:S(2)}, u32[]{:S(2)}) collective-permute-start(bf16[1,24,1280]{2,1,0:T(8,128)(2,1)S(1)} %get-tuple-element.25), channel_id=1, source_target_pairs={{0,16},{16,32},{32,48},{48,64},{64,80},{80,96},{96,112},{112,128},... | collective-permute-start | bytes 184328 | tf_op jit(solution)/shard_map/ppermute | solution.py:20
  13.6 4.2 %collective-permute-start.1 = (bf16[1,24,1280]{2,1,0:T(8,128)(2,1)S(1)}, bf16[1,24,1280]{2,1,0:T(8,128)(2,1)S(1)}, u32[]{:S(2)}, u32[]{:S(2)}) collective-permute-start(bf16[1,24,1280]{2,1,0:T(8,128)(2,1)S(1)} %get-tuple-element.24), channel_id=1, source_target_pairs={{16,0},{32,16},{48,32},{64,48},{80,64},{96,80},{112,96},{128,112},... | collective-permute-start | bytes 184328 | tf_op jit(solution)/shard_map/ppermute | solution.py:22
  17.8 0.0 collective-permute-done
  17.8 0.0 copy-done
  17.8 0.1 constant_dynamic-update-slice_fusion.1
  17.9 1.1 collective-permute-done.1
  19.1 0.2 fusion.19
  19.3 4.8 %collective-permute-start.2 = (bf16[26,1,1280]{2,1,0:T(2,128)(2,1)S(1)}, bf16[26,1,1280]{2,1,0:T(2,128)(2,1)S(1)}, u32[]{:S(2)}, u32[]{:S(2)}) collective-permute-start(bf16[26,1,1280]{2,1,0:T(2,128)(2,1)S(1)} %get-tuple-element.22), channel_id=1, source_target_pairs={{0,1},{1,2},{2,3},{3,4},{4,5},{5,6},{6,7},{7,8},{8,9},{9,10},{10,1... | collective-permute-start | bytes 199688 | tf_op jit(solution)/shard_map/ppermute | solution.py:20
  24.1 1.9 collective-permute-start.3
  26.0 0.0 copy-done.2
  26.0 0.1 slice_reduce_fusion.8
  26.2 0.5 collective-permute-done.2
  26.6 6.8 %collective-permute-done.3 = bf16[26,1,1280]{2,1,0:T(2,128)(2,1)S(1)} collective-permute-done((bf16[26,1,1280]{2,1,0:T(2,128)(2,1)S(1)}, bf16[26,1,1280]{2,1,0:T(2,128)(2,1)S(1)}, u32[]{:S(2)}, u32[]{:S(2)}) %collective-permute-start.3) | collective-permute-done | bytes 66592 | tf_op jit(solution)/shard_map/ppermute | solution.py:22
  33.4 0.0 copy-done.3
  33.4 6.0 %fusion.17 = (f32[24,24]{1,0:T(8,128)S(1)}, f32[24,24,1280]{2,1,0:T(8,128)S(1)}) fusion(bf16[26,1,1280]{2,1,0:T(2,128)(2,1)S(1)} %collective-permute-done.3, bf16[26,24,1280]{2,1,0:T(8,128)(2,1)S(1)} %constant_dynamic-update-slice_fusion, f32[1280]{0:T(1024)S(1)} %get-tuple-element.16, bf16[1,24,1280]{2,1,0:T(8,128)(2,1)S(1)} %collective-permute-done.1, ...), kind=kLoop, calls=%fused_computation.54 | loop fusion | flops 39075264 | bytes 6330624 | tf_op jit(solution)/shard_map/reduce_sum | solution.py:53
  39.4 0.0 copy-start.4
  39.4 0.0 copy-start.5
  39.4 0.4 multiply_reduce_fusion
  39.9 0.2 copy-done.4
  40.1 0.0 copy-done.5
  40.1 1.7 add_convert_fusion.2
  41.8 11.1 %all-gather.2.cloned.1.call-done = bf16[3,1281,640]{1,2,0:T(8,128)(2,1)} async-done(((bf16[3,1281,80]{1,2,0:T(8,128)(2,1)}), bf16[3,1281,640]{1,2,0:T(8,128)(2,1)}) %all-gather.2.cloned.1.call-update) | async-done | bytes 4919056 | tf_op jit(solution)/shard_map/all_gather | solution.py:41
  52.9 1.2 convert_reduce_fusion
  54.1 0.1 reshape.31
  54.2 2.7 %slice.110 = bf16[3,1280,640]{1,2,0:T(8,128)(2,1)S(1)} slice(bf16[3,1281,640]{1,2,0:T(8,128)(2,1)} %all-gather.2.cloned.1.call-done), slice={[0:3], [0:1280], [0:640]} | slice | bytes 9830400 | tf_op jit(solution)/shard_map/slice | solution.py:43
  56.9 0.0 copy-start.1
  56.9 6.7 %fusion = bf16[3,24,8,24,80]{4,3,1,2,0:T(8,128)(2,1)S(1)} fusion(f32[3,8,80]{2,1,0:T(8,128)S(1)} %reshape.31, bf16[3,1280,8,80,1]{1,3,4,2,0:T(8,128)(2,1)S(1)} %bitcast.29, bf16[24,24,1280]{2,1,0:T(8,128)(2,1)} %add_convert_fusion.2), kind=kOutput, calls=%fused_computation.5 | convolution fusion | flops 2833367040 | bytes 8609280 | tf_op jit(solution)/shard_map/rcd,tdhe->trhce/dot_general | solution.py:30
  63.6 0.0 copy-done.1
  63.6 5.6 %collective-permute-start.4 = (bf16[24,24,1280]{2,1,0:T(8,128)(2,1)}, bf16[24,24,1280]{2,1,0:T(8,128)(2,1)}, u32[]{:S(2)}, u32[]{:S(2)}) collective-permute-start(bf16[24,24,1280]{2,1,0:T(8,128)(2,1)} %add_convert_fusion.2), channel_id=1, source_target_pairs={{0,8},{8,0},{1,9},{9,1},{2,10},{10,2},{3,11},{11,3},{4,12},{12,4},... | collective-permute-start | bytes 4423688 | tf_op jit(solution)/shard_map/ppermute | solution.py:58
  69.2 2.4 %copy.13 = bf16[3,24,8,24,80]{4,3,1,0,2:T(8,128)(2,1)} copy(bf16[3,24,8,24,80]{4,3,1,2,0:T(8,128)(2,1)S(1)} %fusion) | data formatting | bytes 4423680 | tf_op jit(solution)/shard_map/optimization_barrier | solution.py:57
  71.6 4.1 %all-to-all-start = ((bf16[3,24,8,24,80]{4,3,1,0,2:T(8,128)(2,1)}), bf16[3,24,8,24,80]{4,3,1,0,2:T(8,128)(2,1)S(1)}, u32[]{:S(2)}, u32[]{:S(2)}) async-start(bf16[3,24,8,24,80]{4,3,1,0,2:T(8,128)(2,1)} %copy.13), calls=%async_computation | async-start | bytes 7077888 | tf_op jit(solution)/shard_map/all_to_all | solution.py:35
  75.7 57.7 %collective-permute-done.4 = bf16[24,24,1280]{2,1,0:T(8,128)(2,1)} collective-permute-done((bf16[24,24,1280]{2,1,0:T(8,128)(2,1)}, bf16[24,24,1280]{2,1,0:T(8,128)(2,1)}, u32[]{:S(2)}, u32[]{:S(2)}) %collective-permute-start.4) | collective-permute-done | bytes 1474592 | tf_op jit(solution)/shard_map/ppermute | solution.py:58
  133.5 7.1 %fusion.1 = bf16[3,24,8,24,80]{4,3,1,2,0:T(8,128)(2,1)S(1)} fusion(f32[3,8,80]{2,1,0:T(8,128)S(1)} %reshape.31, bf16[3,1280,8,80,1]{1,3,4,2,0:T(8,128)(2,1)} %bitcast.30, bf16[24,24,1280]{2,1,0:T(8,128)(2,1)} %collective-permute-done.4), kind=kOutput, calls=%fused_computation.6 | convolution fusion | flops 2833367040 | bytes 8609280 | tf_op jit(solution)/shard_map/rcd,tdhe->trhce/dot_general | solution.py:30
  140.6 2.4 %copy.14 = bf16[3,24,8,24,80]{4,3,1,0,2:T(8,128)(2,1)} copy(bf16[3,24,8,24,80]{4,3,1,2,0:T(8,128)(2,1)S(1)} %fusion.1) | data formatting | bytes 4423680 | tf_op jit(solution)/shard_map/convert_element_type | solution.py:31
  143.0 0.0 all-to-all-done
  143.0 5.5 %all-to-all-start.1 = ((bf16[3,24,8,24,80]{4,3,1,0,2:T(8,128)(2,1)}), bf16[3,24,8,24,80]{4,3,1,0,2:T(8,128)(2,1)}, u32[]{:S(2)}, u32[]{:S(2)}) async-start(bf16[3,24,8,24,80]{4,3,1,0,2:T(8,128)(2,1)} %copy.14), calls=%async_computation.1 | async-start | bytes 7077888 | tf_op jit(solution)/shard_map/all_to_all | solution.py:35
  148.5 41.9 %all-to-all-done.1 = bf16[3,24,8,24,80]{4,3,1,0,2:T(8,128)(2,1)} async-done(((bf16[3,24,8,24,80]{4,3,1,0,2:T(8,128)(2,1)}), bf16[3,24,8,24,80]{4,3,1,0,2:T(8,128)(2,1)}, u32[]{:S(2)}, u32[]{:S(2)}) %all-to-all-start.1) | async-done | bytes 2211872 | tf_op jit(solution)/shard_map/all_to_all | solution.py:35
  190.4 2.5 %select_bitcast_fusion.1 = (bf16[3,24,1,8,24,80]{5,4,1,0,3,2:T(8,128)(2,1)S(1)}, bf16[3,24,1,8,24,80]{5,4,1,0,3,2:T(8,128)(2,1)S(1)}) fusion(bf16[3,24,8,24,80]{4,3,1,0,2:T(8,128)(2,1)S(1)} %all-to-all-done, bf16[3,24,8,24,80]{4,3,1,0,2:T(8,128)(2,1)} %all-to-all-done.1, pred[]{:T(512)S(6)} %eq.3), kind=kLoop, calls=%fused_computation.8 | loop fusion | flops 2211840 | bytes 8847361 | tf_op jit(solution)/shard_map/stack | solution.py:64
  192.9 1.6 pad_maximum_fusion
  194.5 5.0 %copy.15 = bf16[3,24,2,8,24,80]{5,4,3,2,1,0:T(8,128)(2,1)} copy(bf16[3,24,2,8,24,80]{5,4,1,0,3,2:T(8,128)(2,1)S(1)} %pad_maximum_fusion) | data formatting | bytes 8847360 | tf_op jit(solution)/shard_map/stack | solution.py:64
  199.4 13.7 %reshape.30 = bf16[3,1,24,30720]{3,2,0,1:T(8,128)(2,1)} reshape(bf16[3,24,2,8,24,80]{5,4,3,2,1,0:T(8,128)(2,1)} %copy.15) | data formatting | bytes 8847360 | tf_op jit(solution)/shard_map/reshape | solution.py:65
  (4 shorter events, 0.0 us)
Async XLA Ops:
  6.5 11.3 %copy-start = (bf16[24,24,1280]{2,1,0:T(8,128)(2,1)S(1)}, bf16[24,24,1280]{2,1,0:T(8,128)(2,1)}, u32[]{:S(2)}) copy-start(bf16[24,24,1280]{2,1,0:T(8,128)(2,1)} %param.7) | copy-start | bytes 4423684
  6.5 46.4 %all-gather.2.cloned.1.call-start = ((), (), s32[]{:S(2)}) async-start(), calls=%async_computation.2 | async-start | bytes 6082560 | tf_op jit(solution)/shard_map/all_gather | solution.py:41
  7.5 18.6 %copy-start.2 = (f32[3,3,1280]{2,1,0:T(4,128)S(1)}, f32[3,3,1280]{2,1,0:T(4,128)}, u32[]{:S(2)}) copy-start(f32[3,3,1280]{2,1,0:T(4,128)} %param.8) | copy-start | bytes 138244
  7.5 25.9 %copy-start.3 = (f32[1280]{0:T(1024)S(1)}, f32[1280]{0:T(1024)}, u32[]{:S(2)}) copy-start(f32[1280]{0:T(1024)} %param.9) | copy-start | bytes 15364
  10.4 7.4 %collective-permute-start = (bf16[1,24,1280]{2,1,0:T(8,128)(2,1)S(1)}, bf16[1,24,1280]{2,1,0:T(8,128)(2,1)S(1)}, u32[]{:S(2)}, u32[]{:S(2)}) collective-permute-start(bf16[1,24,1280]{2,1,0:T(8,128)(2,1)S(1)} %get-tuple-element.25), channel_id=1, source_target_pairs={{0,16},{16,32},{32,48},{48,64},{64,80},{80,96},{96,112},{112,128},... | collective-permute-start | bytes 184328 | tf_op jit(solution)/shard_map/ppermute | solution.py:20
  13.6 5.5 %collective-permute-start.1 = (bf16[1,24,1280]{2,1,0:T(8,128)(2,1)S(1)}, bf16[1,24,1280]{2,1,0:T(8,128)(2,1)S(1)}, u32[]{:S(2)}, u32[]{:S(2)}) collective-permute-start(bf16[1,24,1280]{2,1,0:T(8,128)(2,1)S(1)} %get-tuple-element.24), channel_id=1, source_target_pairs={{16,0},{32,16},{48,32},{64,48},{80,64},{96,80},{112,96},{128,112},... | collective-permute-start | bytes 184328 | tf_op jit(solution)/shard_map/ppermute | solution.py:22
  19.3 7.3 %collective-permute-start.2 = (bf16[26,1,1280]{2,1,0:T(2,128)(2,1)S(1)}, bf16[26,1,1280]{2,1,0:T(2,128)(2,1)S(1)}, u32[]{:S(2)}, u32[]{:S(2)}) collective-permute-start(bf16[26,1,1280]{2,1,0:T(2,128)(2,1)S(1)} %get-tuple-element.22), channel_id=1, source_target_pairs={{0,1},{1,2},{2,3},{3,4},{4,5},{5,6},{6,7},{7,8},{8,9},{9,10},{10,1... | collective-permute-start | bytes 199688 | tf_op jit(solution)/shard_map/ppermute | solution.py:20
  24.1 9.3 %collective-permute-start.3 = (bf16[26,1,1280]{2,1,0:T(2,128)(2,1)S(1)}, bf16[26,1,1280]{2,1,0:T(2,128)(2,1)S(1)}, u32[]{:S(2)}, u32[]{:S(2)}) collective-permute-start(bf16[26,1,1280]{2,1,0:T(2,128)(2,1)S(1)} %get-tuple-element.23), channel_id=1, source_target_pairs={{1,0},{2,1},{3,2},{4,3},{5,4},{6,5},{7,6},{8,7},{9,8},{10,9},{11,1... | collective-permute-start | bytes 199688 | tf_op jit(solution)/shard_map/ppermute | solution.py:22
  39.4 0.7 copy-start.4
  39.4 0.7 copy-start.5
  56.9 6.7 %copy-start.1 = (bf16[3,1280,640]{1,2,0:T(8,128)(2,1)}, bf16[3,1280,640]{1,2,0:T(8,128)(2,1)S(1)}, u32[]{:S(2)}) copy-start(bf16[3,1280,640]{1,2,0:T(8,128)(2,1)S(1)} %slice.110) | copy-start | bytes 14745604
  63.6 69.8 %collective-permute-start.4 = (bf16[24,24,1280]{2,1,0:T(8,128)(2,1)}, bf16[24,24,1280]{2,1,0:T(8,128)(2,1)}, u32[]{:S(2)}, u32[]{:S(2)}) collective-permute-start(bf16[24,24,1280]{2,1,0:T(8,128)(2,1)} %add_convert_fusion.2), channel_id=1, source_target_pairs={{0,8},{8,0},{1,9},{9,1},{2,10},{10,2},{3,11},{11,3},{4,12},{12,4},... | collective-permute-start | bytes 4423688 | tf_op jit(solution)/shard_map/ppermute | solution.py:58
  71.6 71.4 %all-to-all-start = ((bf16[3,24,8,24,80]{4,3,1,0,2:T(8,128)(2,1)}), bf16[3,24,8,24,80]{4,3,1,0,2:T(8,128)(2,1)S(1)}, u32[]{:S(2)}, u32[]{:S(2)}) async-start(bf16[3,24,8,24,80]{4,3,1,0,2:T(8,128)(2,1)} %copy.13), calls=%async_computation | async-start | bytes 7077888 | tf_op jit(solution)/shard_map/all_to_all | solution.py:35
  143.0 47.4 %all-to-all-start.1 = ((bf16[3,24,8,24,80]{4,3,1,0,2:T(8,128)(2,1)}), bf16[3,24,8,24,80]{4,3,1,0,2:T(8,128)(2,1)}, u32[]{:S(2)}, u32[]{:S(2)}) async-start(bf16[3,24,8,24,80]{4,3,1,0,2:T(8,128)(2,1)} %copy.14), calls=%async_computation.1 | async-start | bytes 7077888 | tf_op jit(solution)/shard_map/all_to_all | solution.py:35
Sparse Core Ops, SparseCore 0:
  9.6 43.2 all-gather.1

commit v3 on v2

--- a/solution.py
+++ b/solution.py
@@ -28,7 +28,8 @@
 
 def project(tile, weight_side, bias_side):
     out = jnp.einsum("rcd,tdhe->trhce", tile, weight_side, preferred_element_type=jnp.float32)
-    return (out + bias_side).astype(jnp.bfloat16)
+    out = (out + bias_side).astype(jnp.bfloat16)
+    return out.reshape(out.shape[:3] + (-1,))
 
 
 def deliver(out):
@@ -53,15 +54,15 @@
     mean = jnp.mean(mixed, axis=-1, keepdims=True)
     var = jnp.mean((mixed - mean) ** 2, axis=-1, keepdims=True)
     normed = ((mixed - mean) / jnp.sqrt(var + 1e-06) * norm_gain + norm_bias).astype(jnp.bfloat16)
+    partner = lax.ppermute(normed, "zh", [(0, 1), (1, 0)])
     own = project(normed, weight_side, bias_side)
-    normed, own = lax.optimization_barrier((normed, own))
-    partner = lax.ppermute(normed, "zh", [(0, 1), (1, 0)])
+    weight_late, bias_late, own = lax.optimization_barrier((weight_side, bias_side, own))
     own = deliver(own)
-    other = deliver(project(partner, weight_side, bias_side))
-    first = lax.axis_index("zh") == 0
-    low = jnp.where(first, own, other)
-    high = jnp.where(first, other, own)
-    got = jnp.stack([low, high], axis=2)
+    other = deliver(project(partner, weight_late, bias_late))
+    me = lax.axis_index("zh")
+    got = jnp.zeros(own.shape[:2] + (2,) + own.shape[2:], own.dtype)
+    got = lax.dynamic_update_slice_in_dim(got, own[:, :, None], me, axis=2)
+    got = lax.dynamic_update_slice_in_dim(got, other[:, :, None], 1 - me, axis=2)
     return got.reshape(3, 1, tile_rows, -1)
 
 

time: 222 us -> 182 us (0.82)
  waiting for transfers between devices: 119 us -> 69.9 us
  local copies, waits for them, and re-layouts: 28.8 us -> 37.4 us
  other arithmetic: 15.4 us -> 11.3 us
  starting transfers between devices: 29.3 us -> 31.6 us
    ppermute x1, waiting for transfers between devices: 57.7 us -> 32.9 us  [local(): partner = lax.ppermute(normed, 'zh', [(0, 1), (1, 0)])]
    all_to_all x2, waiting for transfers between devices: 41.9 us -> 23.7 us  [deliver(): return lax.all_to_all(out, SIDE, 2, 2, tiled=True)]
    reshape x0 -> x3, local copies, waits for them, and re-layouts: none -> 14.6 us  [project(): return out.reshape(out.shape[:3] + (-1,))]
    reshape x1, local copies, waits for them, and re-layouts: 13.7 us -> 6.46 us  [local(): return got.reshape(3, 1, tile_rows, -1)]
    all_gather x1, waiting for transfers between devices: 11.1 us -> 4.87 us  [local(): packed = lax.all_gather(packed, SIDE, axis=2, tiled=True)]
    another operation x1 -> x0, local copies, waits for them, and re-layouts: 4.97 us -> none  [local(): got = jnp.stack([low, high], axis=2)]
    dynamic_update_slice x0 -> x2, local copies, waits for them, and re-layouts: none -> 4.92 us  [the longest x1 3.26 us: local(): lax.dynamic_update_slice_in_dim(got, other[:, :, None], 1 - me, axis=2)]
    another operation x2 -> x0, other arithmetic: 4.05 us -> none  [local(): got = jnp.stack([low, high], axis=2)]
  transfers between devices with their start and end apart: 8 -> 8, of which waited for: 6 -> 6; matrix products, arithmetic and copies ran while one was open for 10% -> 28% of each run, Pallas kernels for 0% -> 0%
where the time goes in v3:
time: 182 us; the launch traced here: 180 us
  waiting for transfers between devices  69.9 us (38%)
  local copies, waits for them, and re-layouts  37.4 us (21%)
  starting transfers between devices  31.6 us (17%)
  matrix products  15.9 us (9%)
  between operations  13.6 us (7%)
  other arithmetic  11.3 us (6%)
    ppermute x1, waiting for transfers between devices, local(): partner = lax.ppermute(normed, 'zh', [(0, 1), (1, 0)])  32.9 us
    all_to_all x2, waiting for transfers between devices, deliver(): return lax.all_to_all(out, SIDE, 2, 2, tiled=True)  23.7 us
    dot_general x2, matrix products, project(): jnp.einsum('rcd,tdhe->trhce', tile, weight_side, preferred_element_type=j...  15.9 us
    reshape x3, local copies, waits for them, and re-layouts, project(): return out.reshape(out.shape[:3] + (-1,))  14.6 us
    all_to_all x2, starting transfers between devices, deliver(): return lax.all_to_all(out, SIDE, 2, 2, tiled=True)  11.3 us
    ppermute x2, starting transfers between devices, with_halo(): lax.ppermute(tail, axis, [(i, (i + 1) % count) for i in range(ends)])  8.02 us
    ppermute x2, waiting for transfers between devices, with_halo(): lax.ppermute(head, axis, [((i + 1) % count, i) for i in range(ends)])  7.92 us
    reshape x1, local copies, waits for them, and re-layouts, local(): return got.reshape(3, 1, tile_rows, -1)  6.46 us
  transfers between devices with their start and end apart: 8, of which 6 were waited for; matrix products, arithmetic and copies ran while one was open for 28% of the time, Pallas kernels for 0%

profile of v3, /device:TPU:33, one launch (start us, length us, event | category | flops | bytes accessed | tf_op | source)
XLA Modules:
  0.0 179.7 jit_solution(6630934312548662887)
XLA Ops:
  6.5 0.0 copy-start
  6.5 0.0 all-gather.2.cloned.1.call-start
  6.5 0.9 copy.14
  7.5 0.0 copy-start.2
  7.5 0.0 copy-start.3
  7.5 2.0 %pad_maximum_fusion.4 = bf16[3,1281,80]{1,2,0:T(8,128)(2,1)} fusion(bf16[3,1,80]{1,2,0:T(8,128)(2,1)S(1)} %copy.14, bf16[3,1280,80]{1,2,0:T(8,128)(2,1)} %param.12), kind=kLoop, calls=%fused_computation.40 | loop fusion | flops 1229760 | bytes 1229760 | tf_op jit(solution)/shard_map/concatenate | solution.py:41
  9.5 0.0 all-gather.2.cloned.1.call-update
  9.5 0.9 fusion.24
  10.4 3.2 %collective-permute-start = (bf16[1,24,1280]{2,1,0:T(8,128)(2,1)S(1)}, bf16[1,24,1280]{2,1,0:T(8,128)(2,1)S(1)}, u32[]{:S(2)}, u32[]{:S(2)}) collective-permute-start(bf16[1,24,1280]{2,1,0:T(8,128)(2,1)S(1)} %get-tuple-element.25), channel_id=1, source_target_pairs={{0,16},{16,32},{32,48},{48,64},{64,80},{80,96},{96,112},{112,128},... | collective-permute-start | bytes 184328 | tf_op jit(solution)/shard_map/ppermute | solution.py:20
  13.6 4.2 %collective-permute-start.1 = (bf16[1,24,1280]{2,1,0:T(8,128)(2,1)S(1)}, bf16[1,24,1280]{2,1,0:T(8,128)(2,1)S(1)}, u32[]{:S(2)}, u32[]{:S(2)}) collective-permute-start(bf16[1,24,1280]{2,1,0:T(8,128)(2,1)S(1)} %get-tuple-element.24), channel_id=1, source_target_pairs={{16,0},{32,16},{48,32},{64,48},{80,64},{96,80},{112,96},{128,112},... | collective-permute-start | bytes 184328 | tf_op jit(solution)/shard_map/ppermute | solution.py:22
  17.8 0.0 collective-permute-done
  17.8 0.0 copy-done
  17.8 0.1 constant_dynamic-update-slice_fusion.1
  17.9 1.1 collective-permute-done.1
  19.1 0.2 fusion.23
  19.3 4.8 %collective-permute-start.2 = (bf16[26,1,1280]{2,1,0:T(2,128)(2,1)S(1)}, bf16[26,1,1280]{2,1,0:T(2,128)(2,1)S(1)}, u32[]{:S(2)}, u32[]{:S(2)}) collective-permute-start(bf16[26,1,1280]{2,1,0:T(2,128)(2,1)S(1)} %get-tuple-element.22), channel_id=1, source_target_pairs={{0,1},{1,2},{2,3},{3,4},{4,5},{5,6},{6,7},{7,8},{8,9},{9,10},{10,1... | collective-permute-start | bytes 199688 | tf_op jit(solution)/shard_map/ppermute | solution.py:20
  24.1 1.9 %collective-permute-start.3 = (bf16[26,1,1280]{2,1,0:T(2,128)(2,1)S(1)}, bf16[26,1,1280]{2,1,0:T(2,128)(2,1)S(1)}, u32[]{:S(2)}, u32[]{:S(2)}) collective-permute-start(bf16[26,1,1280]{2,1,0:T(2,128)(2,1)S(1)} %get-tuple-element.23), channel_id=1, source_target_pairs={{1,0},{2,1},{3,2},{4,3},{5,4},{6,5},{7,6},{8,7},{9,8},{10,9},{11,1... | collective-permute-start | bytes 199688 | tf_op jit(solution)/shard_map/ppermute | solution.py:22
  26.0 0.0 copy-done.2
  26.0 0.1 slice_reduce_fusion.8
  26.2 0.5 collective-permute-done.2
  26.6 6.8 %collective-permute-done.3 = bf16[26,1,1280]{2,1,0:T(2,128)(2,1)S(1)} collective-permute-done((bf16[26,1,1280]{2,1,0:T(2,128)(2,1)S(1)}, bf16[26,1,1280]{2,1,0:T(2,128)(2,1)S(1)}, u32[]{:S(2)}, u32[]{:S(2)}) %collective-permute-start.3) | collective-permute-done | bytes 66592 | tf_op jit(solution)/shard_map/ppermute | solution.py:22
  33.4 0.0 copy-done.3
  33.4 6.0 %fusion.21 = (f32[24,24]{1,0:T(8,128)S(1)}, f32[24,24,1280]{2,1,0:T(8,128)S(1)}) fusion(bf16[26,1,1280]{2,1,0:T(2,128)(2,1)S(1)} %collective-permute-done.3, bf16[26,24,1280]{2,1,0:T(8,128)(2,1)S(1)} %constant_dynamic-update-slice_fusion, f32[1280]{0:T(1024)S(1)} %get-tuple-element.18, bf16[1,24,1280]{2,1,0:T(8,128)(2,1)S(1)} %collective-permute-done.1, ...), kind=kLoop, calls=%fused_computation.55 | loop fusion | flops 39075264 | bytes 6330624 | tf_op jit(solution)/shard_map/reduce_sum | solution.py:54
  39.4 0.0 copy-start.4
  39.4 0.0 copy-start.5
  39.4 0.4 multiply_reduce_fusion
  39.9 0.2 copy-done.4
  40.1 0.0 copy-done.5
  40.1 1.7 add_convert_fusion.2
  41.8 6.2 %collective-permute-start.4 = (bf16[24,24,1280]{2,1,0:T(8,128)(2,1)}, bf16[24,24,1280]{2,1,0:T(8,128)(2,1)}, u32[]{:S(2)}, u32[]{:S(2)}) collective-permute-start(bf16[24,24,1280]{2,1,0:T(8,128)(2,1)} %add_convert_fusion.2), channel_id=1, source_target_pairs={{0,8},{8,0},{1,9},{9,1},{2,10},{10,2},{3,11},{11,3},{4,12},{12,4},... | collective-permute-start | bytes 4423688 | tf_op jit(solution)/shard_map/ppermute | solution.py:57
  48.0 4.9 %all-gather.2.cloned.1.call-done = bf16[3,1281,640]{1,2,0:T(8,128)(2,1)} async-done(((bf16[3,1281,80]{1,2,0:T(8,128)(2,1)}), bf16[3,1281,640]{1,2,0:T(8,128)(2,1)}) %all-gather.2.cloned.1.call-update) | async-done | bytes 4919056 | tf_op jit(solution)/shard_map/all_gather | solution.py:42
  52.9 1.2 convert_reduce_fusion
  54.1 0.1 reshape.48
  54.2 0.1 reshape.47
  54.3 2.7 %slice.100 = bf16[3,1280,640]{1,2,0:T(8,128)(2,1)S(1)} slice(bf16[3,1281,640]{1,2,0:T(8,128)(2,1)} %all-gather.2.cloned.1.call-done), slice={[0:3], [0:1280], [0:640]} | slice | bytes 9830400 | tf_op jit(solution)/shard_map/slice | solution.py:44
  57.0 0.0 copy-start.1
  57.0 2.2 %copy-done.1 = bf16[3,1280,640]{1,2,0:T(8,128)(2,1)} copy-done((bf16[3,1280,640]{1,2,0:T(8,128)(2,1)}, bf16[3,1280,640]{1,2,0:T(8,128)(2,1)S(1)}, u32[]{:S(2)}) %copy-start.1) | copy-done | bytes 4915224
  59.2 7.6 %fusion.2 = bf16[3,24,8,24,80]{4,3,1,2,0:T(8,128)(2,1)} fusion(f32[3,8,80]{2,1,0:T(8,128)S(1)} %reshape.48, bf16[3,1280,8,80,1]{1,3,4,2,0:T(8,128)(2,1)S(1)} %bitcast.42, bf16[24,24,1280]{2,1,0:T(8,128)(2,1)} %add_convert_fusion.2), kind=kOutput, calls=%fused_computation.6 | convolution fusion | flops 2833367040 | bytes 8609280 | tf_op jit(solution)/shard_map/rcd,tdhe->trhce/dot_general | solution.py:30
  66.8 5.3 %reshape.44 = bf16[3,24,8,1920]{3,1,2,0:T(8,128)(2,1)S(1)} reshape(bf16[3,24,8,24,80]{4,3,1,2,0:T(8,128)(2,1)} %fusion.2) | data formatting | bytes 4423680 | tf_op jit(solution)/shard_map/reshape | solution.py:32
  72.1 1.5 copy.15
  73.6 4.2 %all-to-all-start = ((bf16[3,24,8,1920]{3,1,0,2:T(8,128)(2,1)}), bf16[3,24,8,1920]{3,1,0,2:T(8,128)(2,1)S(1)}, u32[]{:S(2)}, u32[]{:S(2)}) async-start(bf16[3,24,8,1920]{3,1,0,2:T(8,128)(2,1)} %copy.15), calls=%async_computation | async-start | bytes 4423680 | tf_op jit(solution)/shard_map/all_to_all | solution.py:36
  77.8 32.9 %collective-permute-done.4 = bf16[24,24,1280]{2,1,0:T(8,128)(2,1)} collective-permute-done((bf16[24,24,1280]{2,1,0:T(8,128)(2,1)}, bf16[24,24,1280]{2,1,0:T(8,128)(2,1)}, u32[]{:S(2)}, u32[]{:S(2)}) %collective-permute-start.4) | collective-permute-done | bytes 1474592 | tf_op jit(solution)/shard_map/ppermute | solution.py:57
  110.7 8.3 %fusion.3 = bf16[3,24,8,24,80]{4,3,1,2,0:T(8,128)(2,1)} fusion(f32[3,8,80]{2,1,0:T(8,128)S(1)} %bitcast.44, bf16[3,1280,8,80]{1,3,2,0:T(8,128)(2,1)} %bitcast.43, bf16[24,24,1280]{2,1,0:T(8,128)(2,1)} %collective-permute-done.4), kind=kOutput, calls=%fused_computation.7 | convolution fusion | flops 2833367040 | bytes 8609280 | tf_op jit(solution)/shard_map/rcd,tdhe->trhce/dot_general | solution.py:30
  119.1 6.2 %reshape.45 = bf16[3,24,8,1920]{3,1,2,0:T(8,128)(2,1)} reshape(bf16[3,24,8,24,80]{4,3,1,2,0:T(8,128)(2,1)} %fusion.3) | data formatting | bytes 4423680 | tf_op jit(solution)/shard_map/reshape | solution.py:32
  125.3 3.1 %copy.17 = bf16[3,24,8,1920]{3,1,0,2:T(8,128)(2,1)} copy(bf16[3,24,8,1920]{3,1,2,0:T(8,128)(2,1)} %reshape.45) | data formatting | bytes 4423680 | tf_op jit(solution)/shard_map/reshape | solution.py:32
  128.4 0.0 all-to-all-done
  128.4 7.0 %all-to-all-start.1 = ((bf16[3,24,8,1920]{3,1,0,2:T(8,128)(2,1)}), bf16[3,24,8,1920]{3,1,0,2:T(8,128)(2,1)}, u32[]{:S(2)}, u32[]{:S(2)}) async-start(bf16[3,24,8,1920]{3,1,0,2:T(8,128)(2,1)} %copy.17), calls=%async_computation.1 | async-start | bytes 4423680 | tf_op jit(solution)/shard_map/all_to_all | solution.py:36
  135.5 2.3 %broadcast_in_dim.8 = bf16[3,24,2,8,1920]{4,3,2,1,0:T(8,128)(2,1)} broadcast(bf16[]{:T(256)} %constant.5.clone.1), dimensions={} | broadcast | bytes 4423682 | tf_op jit(solution)/shard_map/broadcast_in_dim | solution.py:63
  137.8 1.7 copy_dynamic-update-slice_fusion.1
  139.5 23.7 %all-to-all-done.1 = bf16[3,24,8,1920]{3,1,0,2:T(8,128)(2,1)} async-done(((bf16[3,24,8,1920]{3,1,0,2:T(8,128)(2,1)}), bf16[3,24,8,1920]{3,1,0,2:T(8,128)(2,1)}, u32[]{:S(2)}, u32[]{:S(2)}) %all-to-all-start.1) | async-done | bytes 2211872 | tf_op jit(solution)/shard_map/all_to_all | solution.py:36
  163.2 3.3 %copy_dynamic-update-slice_fusion = bf16[3,24,2,8,1920]{4,3,2,1,0:T(8,128)(2,1)} fusion(bf16[3,24,2,8,1920]{4,3,2,1,0:T(8,128)(2,1)} %copy_dynamic-update-slice_fusion.1, s32[]{:T(128)S(6)} %select_n.7, bf16[3,24,1,8,1920]{4,1,0,3,2:T(8,128)(2,1)} %bitcast.14), kind=kLoop, calls=%fused_computation.23 | loop fusion | bytes 4423684 | tf_op jit(solution)/shard_map/dynamic_update_slice | solution.py:65
  166.4 6.5 %reshape.46 = bf16[3,1,24,30720]{3,2,1,0:T(8,128)(2,1)} reshape(bf16[3,24,2,8,1920]{4,3,2,1,0:T(8,128)(2,1)} %copy_dynamic-update-slice_fusion) | data formatting | bytes 8847360 | tf_op jit(solution)/shard_map/reshape | solution.py:66
  (4 shorter events, 0.0 us)
Async XLA Ops:
  6.5 11.3 %copy-start = (bf16[24,24,1280]{2,1,0:T(8,128)(2,1)S(1)}, bf16[24,24,1280]{2,1,0:T(8,128)(2,1)}, u32[]{:S(2)}) copy-start(bf16[24,24,1280]{2,1,0:T(8,128)(2,1)} %param.7) | copy-start | bytes 4423684
  6.5 46.4 %all-gather.2.cloned.1.call-start = ((), (), s32[]{:S(2)}) async-start(), calls=%async_computation.2 | async-start | bytes 6082560 | tf_op jit(solution)/shard_map/all_gather | solution.py:42
  7.5 18.6 %copy-start.2 = (f32[3,3,1280]{2,1,0:T(4,128)S(1)}, f32[3,3,1280]{2,1,0:T(4,128)}, u32[]{:S(2)}) copy-start(f32[3,3,1280]{2,1,0:T(4,128)} %param.8) | copy-start | bytes 138244
  7.5 25.9 %copy-start.3 = (f32[1280]{0:T(1024)S(1)}, f32[1280]{0:T(1024)}, u32[]{:S(2)}) copy-start(f32[1280]{0:T(1024)} %param.9) | copy-start | bytes 15364
  10.4 7.4 %collective-permute-start = (bf16[1,24,1280]{2,1,0:T(8,128)(2,1)S(1)}, bf16[1,24,1280]{2,1,0:T(8,128)(2,1)S(1)}, u32[]{:S(2)}, u32[]{:S(2)}) collective-permute-start(bf16[1,24,1280]{2,1,0:T(8,128)(2,1)S(1)} %get-tuple-element.25), channel_id=1, source_target_pairs={{0,16},{16,32},{32,48},{48,64},{64,80},{80,96},{96,112},{112,128},... | collective-permute-start | bytes 184328 | tf_op jit(solution)/shard_map/ppermute | solution.py:20
  13.6 5.5 %collective-permute-start.1 = (bf16[1,24,1280]{2,1,0:T(8,128)(2,1)S(1)}, bf16[1,24,1280]{2,1,0:T(8,128)(2,1)S(1)}, u32[]{:S(2)}, u32[]{:S(2)}) collective-permute-start(bf16[1,24,1280]{2,1,0:T(8,128)(2,1)S(1)} %get-tuple-element.24), channel_id=1, source_target_pairs={{16,0},{32,16},{48,32},{64,48},{80,64},{96,80},{112,96},{128,112},... | collective-permute-start | bytes 184328 | tf_op jit(solution)/shard_map/ppermute | solution.py:22
  19.3 7.3 %collective-permute-start.2 = (bf16[26,1,1280]{2,1,0:T(2,128)(2,1)S(1)}, bf16[26,1,1280]{2,1,0:T(2,128)(2,1)S(1)}, u32[]{:S(2)}, u32[]{:S(2)}) collective-permute-start(bf16[26,1,1280]{2,1,0:T(2,128)(2,1)S(1)} %get-tuple-element.22), channel_id=1, source_target_pairs={{0,1},{1,2},{2,3},{3,4},{4,5},{5,6},{6,7},{7,8},{8,9},{9,10},{10,1... | collective-permute-start | bytes 199688 | tf_op jit(solution)/shard_map/ppermute | solution.py:20
  24.1 9.3 %collective-permute-start.3 = (bf16[26,1,1280]{2,1,0:T(2,128)(2,1)S(1)}, bf16[26,1,1280]{2,1,0:T(2,128)(2,1)S(1)}, u32[]{:S(2)}, u32[]{:S(2)}) collective-permute-start(bf16[26,1,1280]{2,1,0:T(2,128)(2,1)S(1)} %get-tuple-element.23), channel_id=1, source_target_pairs={{1,0},{2,1},{3,2},{4,3},{5,4},{6,5},{7,6},{8,7},{9,8},{10,9},{11,1... | collective-permute-start | bytes 199688 | tf_op jit(solution)/shard_map/ppermute | solution.py:22
  39.4 0.7 copy-start.4
  39.4 0.7 copy-start.5
  41.8 68.9 %collective-permute-start.4 = (bf16[24,24,1280]{2,1,0:T(8,128)(2,1)}, bf16[24,24,1280]{2,1,0:T(8,128)(2,1)}, u32[]{:S(2)}, u32[]{:S(2)}) collective-permute-start(bf16[24,24,1280]{2,1,0:T(8,128)(2,1)} %add_convert_fusion.2), channel_id=1, source_target_pairs={{0,8},{8,0},{1,9},{9,1},{2,10},{10,2},{3,11},{11,3},{4,12},{12,4},... | collective-permute-start | bytes 4423688 | tf_op jit(solution)/shard_map/ppermute | solution.py:57
  57.0 2.2 %copy-start.1 = (bf16[3,1280,640]{1,2,0:T(8,128)(2,1)}, bf16[3,1280,640]{1,2,0:T(8,128)(2,1)S(1)}, u32[]{:S(2)}) copy-start(bf16[3,1280,640]{1,2,0:T(8,128)(2,1)S(1)} %slice.100) | copy-start | bytes 14745604
  73.6 54.8 %all-to-all-start = ((bf16[3,24,8,1920]{3,1,0,2:T(8,128)(2,1)}), bf16[3,24,8,1920]{3,1,0,2:T(8,128)(2,1)S(1)}, u32[]{:S(2)}, u32[]{:S(2)}) async-start(bf16[3,24,8,1920]{3,1,0,2:T(8,128)(2,1)} %copy.15), calls=%async_computation | async-start | bytes 4423680 | tf_op jit(solution)/shard_map/all_to_all | solution.py:36
  128.4 34.7 %all-to-all-start.1 = ((bf16[3,24,8,1920]{3,1,0,2:T(8,128)(2,1)}), bf16[3,24,8,1920]{3,1,0,2:T(8,128)(2,1)}, u32[]{:S(2)}, u32[]{:S(2)}) async-start(bf16[3,24,8,1920]{3,1,0,2:T(8,128)(2,1)} %copy.17), calls=%async_computation.1 | async-start | bytes 4423680 | tf_op jit(solution)/shard_map/all_to_all | solution.py:36
Sparse Core Ops, SparseCore 0:
  9.6 43.2 all-gather.1
